TPU v7x, 128 devices: a whole 4x4x4 slice. The times are simulated.
128 devices in a mesh: row: 8 (over x, core), col: 16 (over y, z).
Axes of the slice: x: 4, y: 4, z: 4, core: 2. Of those that a mesh axis runs over, the one named last changes fastest.
Arguments:
- trail: bfloat16 [16384, 16384], P('row', 'col'), may hold values from -0.046875 to 0.046875
- row_one: bfloat16 [128, 16384], P('row', 'col'), may hold values from -0.5 to 0.5
- row_two: bfloat16 [128, 16384], P('row', 'col'), may hold values from -0.5 to 0.5
- diag_one: float32 [128, 128], replicated, may hold values from -1 to 2, as said below
- diag_two: float32 [128, 128], replicated, may hold values from -1 to 2, as said below
- adj_trail: float32 [16384, 16384], P('row', 'col'), may hold values from -6 to 6
- adj_row_one: float32 [128, 16384], P('row', 'col'), may hold values from -6 to 6
- adj_row_two: float32 [128, 16384], P('row', 'col'), may hold values from -6 to 6
- adj_diag_one: float32 [128, 128], replicated, may hold values from -6 to 6
- adj_diag_two: float32 [128, 128], replicated, may hold values from -6 to 6
Outputs:
- grad_trail: bfloat16 [16384, 16384], P('row', 'col')
- grad_row_one: float32 [128, 16384], P('row', 'col')
- grad_row_two: float32 [128, 16384], P('row', 'col')
- grad_diag_one: float32 [128, 128], replicated
- grad_diag_two: float32 [128, 128], replicated
Inputs may be any that keep to these rules, and one draw needn't show every extreme that they name: `diag_one`: lower triangular with a positive diagonal. `diag_two`: lower triangular with a positive diagonal.
All inputs are finite; a program needn't handle non-finite values.
Results may differ from a plain program's by a relative error of at most 0.014.
Values may be sent and summed in bfloat16 or wider, within the bound.
A program may use at most 128 MiB of HBM per device.

v0:
```python
import jax
import jax.numpy as jnp
from jax import lax
from jax.sharding import PartitionSpec as P

exact_mode = lax.Precision.HIGHEST


def from_root(value, axis, source):
    kept = jnp.where(lax.axis_index(axis) == source, value, 0).astype(value.dtype)
    return lax.psum(kept, axis)


def halved_lower(matrix):
    order = matrix.shape[0]
    keep = jnp.tril(jnp.ones((order, order), matrix.dtype)) - 0.5 * jnp.eye(
        order, dtype=matrix.dtype
    )
    return matrix * keep


def inverse_lower(block):
    ident = jnp.eye(block.shape[0], dtype=block.dtype)
    return lax.linalg.triangular_solve(block, ident, left_side=True, lower=True)


def block_adjoint(block, inverse, seed_adj):
    inner = halved_lower(jnp.dot(block.T, seed_adj, precision=exact_mode))
    middle = jnp.dot(inverse.T, inner, precision=exact_mode)
    return halved_lower(jnp.dot(middle, inverse, precision=exact_mode))


def per_device(
    trail,
    row_one,
    row_two,
    diag_one,
    diag_two,
    adj_trail,
    adj_row_one,
    adj_row_two,
    adj_diag_one,
    adj_diag_two,
):
    panel = diag_one.shape[0]
    width = trail.shape[1]
    band = row_one.shape[0]
    last = width - panel
    col_count = lax.axis_size("col")
    col_here = lax.axis_index("col")
    row_start = lax.axis_index("row") * band
    here_one = col_here == col_count - 2
    here_two = col_here == col_count - 1
    full_one, full_two = (
        lax.all_gather(row_one, "row", axis=0, tiled=True),
        lax.all_gather(row_two, "row", axis=0, tiled=True),
    )

    def own_rows(matrix):
        return lax.dynamic_slice_in_dim(matrix, row_start, band, 0)

    def solve_panel(rows, inverse, root):
        whole = from_root(rows, "col", root)
        return jnp.dot(whole, inverse, precision=exact_mode).astype(jnp.bfloat16)

    def summed_block(partial_value, root):
        rows_sum = lax.psum(partial_value, "row")
        return from_root(rows_sum, "col", root)

    inverse_two = inverse_lower(diag_two)
    solved_two = solve_panel(adj_trail[:, last:], inverse_two, col_count - 1)
    partial_two = jnp.dot(solved_two.T, trail[:, last:], preferred_element_type=jnp.float32)
    seed_two = jnp.tril(adj_diag_two - summed_block(partial_two, col_count - 1))
    grad_diag_two = block_adjoint(diag_two, inverse_two, seed_two)
    mirror_two = own_rows(grad_diag_two + grad_diag_two.T)
    rest_two = jnp.dot(mirror_two, full_two.astype(jnp.float32), precision=exact_mode)
    inverse_one = inverse_lower(diag_one)
    crossed = lax.psum_scatter(
        jnp.dot(solved_two.T, trail, preferred_element_type=jnp.float32).astype(jnp.bfloat16),
        "row",
        scatter_dimension=0,
        tiled=True,
    ).astype(jnp.float32)
    adj_two = adj_row_two - crossed - rest_two
    adj_next = adj_trail - jnp.dot(solved_two, full_two, preferred_element_type=jnp.float32)
    stacked = jnp.concatenate([adj_two[:, last:], adj_next[:, last:]], 0)
    solved_one = solve_panel(stacked, inverse_one, col_count - 2)
    head_rows = solved_one[:band]
    tail_rows = solved_one[band:]
    partial_one = jnp.dot(
        head_rows.T, row_two[:, last:], preferred_element_type=jnp.float32
    ) + jnp.dot(tail_rows.T, trail[:, last:], preferred_element_type=jnp.float32)
    seed_one = jnp.tril(adj_diag_one - summed_block(partial_one, col_count - 2))
    grad_diag_one = block_adjoint(diag_one, inverse_one, seed_one)
    mirror_one = own_rows(grad_diag_one + grad_diag_one.T)
    rest_one = jnp.dot(mirror_one, full_one.astype(jnp.float32), precision=exact_mode)
    head_update = jnp.dot(head_rows, full_one, preferred_element_type=jnp.float32)
    two_left = adj_two - head_update
    trail_left = adj_next - jnp.dot(tail_rows, full_one, preferred_element_type=jnp.float32)
    crossed_one = lax.psum_scatter(
        (
            jnp.dot(head_rows.T, row_two, preferred_element_type=jnp.float32)
            + jnp.dot(tail_rows.T, trail, preferred_element_type=jnp.float32)
        ).astype(jnp.bfloat16),
        "row",
        scatter_dimension=0,
        tiled=True,
    ).astype(jnp.float32)
    one_left = adj_row_one - crossed_one - rest_one
    trail_block = jnp.where(
        here_one,
        tail_rows.astype(jnp.float32),
        jnp.where(here_two, solved_two.astype(jnp.float32), trail_left[:, last:]),
    )
    grad_trail = jnp.concatenate([trail_left[:, :last], trail_block], 1).astype(jnp.bfloat16)
    zero_block = jnp.zeros((band, panel), jnp.float32)
    one_block = jnp.where(here_one | here_two, zero_block, one_left[:, last:])
    grad_row_one = jnp.concatenate([one_left[:, :last], one_block], 1)
    two_block = jnp.where(
        here_one, head_rows.astype(jnp.float32), jnp.where(here_two, zero_block, two_left[:, last:])
    )
    grad_row_two = jnp.concatenate([two_left[:, :last], two_block], 1)
    return (grad_trail, grad_row_one, grad_row_two, grad_diag_one, grad_diag_two)


def solution(mesh):
    in_specs = (
        P("row", "col"),
        P("row", "col"),
        P("row", "col"),
        P(),
        P(),
        P("row", "col"),
        P("row", "col"),
        P("row", "col"),
        P(),
        P(),
    )
    out_specs = (P("row", "col"), P("row", "col"), P("row", "col"), P(), P())
    return jax.shard_map(
        per_device, mesh=mesh, in_specs=in_specs, out_specs=out_specs, check_vma=False
    )
```

profile of v0, /device:TPU:0, one launch (start us, length us, event | category | flops | bytes accessed | tf_op | source)
XLA Modules:
  0.0 564.0 jit_solution(18032866646956129577)
XLA Ops:
  7.2 0.0 all-reduce.7.cloned.1.call-start
  7.2 2.3 slice_select_fusion.1
  9.5 0.0 all-reduce.7.cloned.1.call-update
  9.5 0.0 all-reduce.9.cloned.1.call-start
  9.6 0.9 select_bitcast_fusion.1
  10.4 9.8 %custom-call.4 = f32[1,128,128]{1,2,0:T(8,128)S(1)} custom-call(f32[1,128,128]{2,1,0:T(8,128)S(1)} %select_bitcast_fusion.1), custom_call_target="InvertDiagBlocksLowerTriangular" | custom-call | tf_op jit(solution)/shard_map/triangular_solve/custom-call.1 | solution.py:24
  20.3 13.5 %all_gather.6 = bf16[128,1024]{1,0:T(8,128)(2,1)S(1)} all-gather(bf16[16,1024]{1,0:T(8,128)(2,1)} %param.14), channel_id=1, replica_groups=mesh['row'=8,'col'=16] {'row'}, dimensions={0}, use_global_device_ids=true | all-gather | bytes 294912 | tf_op jit(solution)/shard_map/all_gather | solution.py:56
  33.7 0.3 fusion.13
  34.0 67.5 %all-reduce.7.cloned.1.call-done = f32[2048,128]{1,0:T(8,128)} async-done(((f32[2048,128]{1,0:T(8,128)}), f32[2048,128]{1,0:T(8,128)}) %all-reduce.7.cloned.1.call-update) | async-done | bytes 1048592 | tf_op jit(solution)/shard_map/psum | solution.py:11
  101.5 2.2 convolution_convert_fusion.1
  103.7 2.0 fusion.6
  105.7 0.0 all-reduce.9.cloned.1.call-update
  105.7 0.0 all-reduce.11.cloned.1.call-start
  105.8 7.9 %convolution_subtract_fusion.1 = f32[2048,1024]{1,0:T(8,128)} fusion(f32[2048,1024]{1,0:T(8,128)} %param.17, bf16[2048,128]{1,0:T(8,128)(2,1)S(1)} %convolution_convert_fusion.1, bf16[128,1024]{1,0:T(8,128)(2,1)S(1)} %all_gather.6), kind=kOutput, calls=%fused_computation.2 | convolution fusion | flops 538968064 | bytes 17563648 | tf_op jit(solution)/shard_map/dot_general | solution.py:85
  113.6 50.0 %all-reduce.9.cloned.1.call-done = f32[128,128]{1,0:T(8,128)} async-done(((f32[128,128]{1,0:T(8,128)}), f32[128,128]{1,0:T(8,128)}) %all-reduce.9.cloned.1.call-update) | async-done | bytes 65552 | tf_op jit(solution)/shard_map/psum | solution.py:67
  163.6 0.6 broadcast_select_fusion.1
  164.2 0.0 all-reduce.11.cloned.1.call-update
  164.3 0.0 reduce-scatter.7.cloned.1.call-start
  164.3 3.7 convolution_convert_fusion.2
  168.0 0.0 reduce-scatter.7.cloned.1.call-update
  168.1 0.0 all-reduce.13.cloned.1.call-start
  168.1 79.6 %all-reduce.11.cloned.1.call-done = f32[128,128]{1,0:T(8,128)} async-done(((f32[128,128]{1,0:T(8,128)}), f32[128,128]{1,0:T(8,128)}) %all-reduce.11.cloned.1.call-update) | async-done | bytes 65552 | tf_op jit(solution)/shard_map/psum | solution.py:11
  247.7 1.1 fusion.2
  248.9 0.3 fusion.42
  249.2 0.2 fusion.25
  249.4 0.1 copy.62
  249.5 30.7 %reduce-scatter.7.cloned.1.call-done = bf16[16,1024]{1,0:T(8,128)(2,1)} async-done(((bf16[128,1024]{1,0:T(8,128)(2,1)}), bf16[16,1024]{1,0:T(8,128)(2,1)}) %reduce-scatter.7.cloned.1.call-update) | async-done | bytes 32784 | tf_op jit(solution)/shard_map/reduce_scatter | solution.py:78
  280.2 1.0 convolution_subtract_fusion.4
  281.2 1.0 maximum_select_fusion
  282.3 0.0 all-reduce.13.cloned.1.call-update
  282.3 0.0 all-reduce.15.cloned.1.call-start
  282.4 9.8 %custom-call.5 = f32[1,128,128]{1,2,0:T(8,128)S(1)} custom-call(f32[1,128,128]{2,1,0:T(8,128)S(1)} %select_bitcast_fusion), custom_call_target="InvertDiagBlocksLowerTriangular" | custom-call | tf_op jit(solution)/shard_map/triangular_solve/custom-call.1 | solution.py:24
  292.2 13.0 %all_gather.7 = bf16[128,1024]{1,0:T(8,128)(2,1)S(1)} all-gather(bf16[16,1024]{1,0:T(8,128)(2,1)S(1)} %copy-done.10), channel_id=1, replica_groups=mesh['row'=8,'col'=16] {'row'}, dimensions={0}, use_global_device_ids=true | all-gather | bytes 294912 | tf_op jit(solution)/shard_map/all_gather | solution.py:55
  305.2 0.3 fusion.11
  305.5 64.7 %all-reduce.13.cloned.1.call-done = f32[2064,128]{1,0:T(8,128)} async-done(((f32[2064,128]{1,0:T(8,128)}), f32[2064,128]{1,0:T(8,128)}) %all-reduce.13.cloned.1.call-update) | async-done | bytes 1056784 | tf_op jit(solution)/shard_map/psum | solution.py:11
  370.2 2.2 convolution_convert_fusion
  372.4 0.2 fusion.32
  372.6 0.2 fusion.36
  372.8 0.2 convolution_subtract_fusion.2
  373.0 6.7 %convolution_subtract_fusion = bf16[2048,1024]{1,0:T(8,128)(2,1)} fusion(f32[2048,1024]{1,0:T(8,128)} %convolution_subtract_fusion.1, bf16[128,1024]{1,0:T(8,128)(2,1)S(1)} %all_gather.7, bf16[2064,128]{1,0:T(8,128)(2,1)S(1)} %convolution_convert_fusion), kind=kOutput, calls=%fused_computation.1 | convolution fusion | flops 541065216 | bytes 13369344 | tf_op jit(solution)/shard_map/dot_general | solution.py:99
  379.7 2.0 convolution_add_fusion.1
  381.7 0.0 all-reduce.15.cloned.1.call-update
  381.7 0.0 all-reduce.17.cloned.1.call-start
  381.7 3.6 fusion
  385.4 1.2 fusion.4
  386.6 0.0 slice-start.1
  386.7 4.1 slice.97
  390.8 48.5 %all-reduce.15.cloned.1.call-done = f32[128,128]{1,0:T(8,128)} async-done(((f32[128,128]{1,0:T(8,128)}), f32[128,128]{1,0:T(8,128)}) %all-reduce.15.cloned.1.call-update) | async-done | bytes 65552 | tf_op jit(solution)/shard_map/psum | solution.py:67
  439.3 0.6 broadcast_select_fusion
  439.9 0.0 all-reduce.17.cloned.1.call-update
  440.0 0.0 reduce-scatter.9.cloned.1.call-start
  440.0 0.6 pad_maximum_fusion.2
  440.6 0.0 reduce-scatter.9.cloned.1.call-update
  440.7 0.0 copy-start.8
  440.7 0.0 copy-start.9
  440.7 4.7 pad_maximum_fusion
  445.4 78.0 %all-reduce.17.cloned.1.call-done = f32[128,128]{1,0:T(8,128)} async-done(((f32[128,128]{1,0:T(8,128)}), f32[128,128]{1,0:T(8,128)}) %all-reduce.17.cloned.1.call-update) | async-done | bytes 65552 | tf_op jit(solution)/shard_map/psum | solution.py:11
  523.4 1.1 fusion.1
  524.6 0.3 fusion.43
  524.8 0.2 fusion.24
  525.1 0.1 copy.67
  525.2 30.3 %reduce-scatter.9.cloned.1.call-done = bf16[16,1024]{1,0:T(8,128)(2,1)} async-done(((bf16[128,1024]{1,0:T(8,128)(2,1)}), bf16[16,1024]{1,0:T(8,128)(2,1)}) %reduce-scatter.9.cloned.1.call-update) | async-done | bytes 32784 | tf_op jit(solution)/shard_map/reduce_scatter | solution.py:100
  555.5 1.0 convolution_subtract_fusion.3
  556.5 0.6 pad_maximum_fusion.1
  (29 shorter events, 0.1 us)
Async XLA Ops:
  7.2 94.3 %all-reduce.7.cloned.1.call-start = ((), (), s32[]{:S(2)}) async-start(), calls=%async_computation.2 | async-start | bytes 2097152 | tf_op jit(solution)/shard_map/psum | solution.py:11
  9.5 154.1 %all-reduce.9.cloned.1.call-start = ((), (), s32[]{:S(2)}) async-start(), calls=%async_computation.3 | async-start | bytes 131072 | tf_op jit(solution)/shard_map/psum | solution.py:67
  105.7 142.0 %all-reduce.11.cloned.1.call-start = ((), (), s32[]{:S(2)}) async-start(), calls=%async_computation.4 | async-start | bytes 131072 | tf_op jit(solution)/shard_map/psum | solution.py:11
  113.6 134.1 %copy-start.1 = (f32[128,128]{1,0:T(8,128)S(1)}, f32[128,128]{1,0:T(8,128)}, u32[]{:S(2)}) copy-start(f32[128,128]{1,0:T(8,128)} %param.16) | copy-start | bytes 196612
  113.6 134.1 %copy-start.6 = (f32[128,128]{1,0:T(8,128)S(1)}, f32[128,128]{1,0:T(8,128)}, u32[]{:S(2)}) copy-start(f32[128,128]{1,0:T(8,128)} %param.21) | copy-start | bytes 196612
  113.6 166.6 %copy-start.7 = (f32[16,1024]{1,0:T(8,128)S(1)}, f32[16,1024]{1,0:T(8,128)}, u32[]{:S(2)}) copy-start(f32[16,1024]{1,0:T(8,128)} %param.19) | copy-start | bytes 196612
  164.3 117.0 %slice-start = ((f32[2048,1024]{1,0:T(8,128)}), f32[2048,128]{1,0:T(8,128)S(1)}, s32[]{:S(2)}) async-start(f32[2048,1024]{1,0:T(8,128)} %convolution_subtract_fusion.1), calls=%async_computation.10 | async-start | bytes 2097152 | tf_op jit(solution)/shard_map/slice | solution.py:86
  164.3 116.0 %reduce-scatter.7.cloned.1.call-start = ((), (), s32[]{:S(2)}) async-start(), calls=%async_computation.8 | async-start | bytes 294912 | tf_op jit(solution)/shard_map/reduce_scatter | solution.py:78
  168.0 114.3 %copy-start.2 = (f32[128,128]{1,0:T(8,128)S(1)}, f32[128,128]{1,0:T(8,128)}, u32[]{:S(2)}) copy-start(f32[128,128]{1,0:T(8,128)} %param.15) | copy-start | bytes 196612
  168.0 124.2 %copy-start.10 = (bf16[16,1024]{1,0:T(8,128)(2,1)S(1)}, bf16[16,1024]{1,0:T(8,128)(2,1)}, u32[]{:S(2)}) copy-start(bf16[16,1024]{1,0:T(8,128)(2,1)} %param.13) | copy-start | bytes 98308
  168.0 204.4 %copy-start.3 = (bf16[16,1024]{1,0:T(8,128)(2,1)S(1)}, bf16[16,1024]{1,0:T(8,128)(2,1)}, u32[]{:S(2)}) copy-start(bf16[16,1024]{1,0:T(8,128)(2,1)} %param.14) | copy-start | bytes 98308
  168.1 202.1 %all-reduce.13.cloned.1.call-start = ((), (), s32[]{:S(2)}) async-start(), calls=%async_computation.5 | async-start | bytes 2113536 | tf_op jit(solution)/shard_map/psum | solution.py:11
  249.4 130.3 %copy-start.4 = (f32[128,128]{1,0:T(8,128)}, f32[128,128]{1,0:T(8,128)S(1)}, u32[]{:S(2)}) copy-start(f32[128,128]{1,0:T(8,128)S(1)} %get-tuple-element.16) | copy-start | bytes 196612
  282.3 157.0 %all-reduce.15.cloned.1.call-start = ((), (), s32[]{:S(2)}) async-start(), calls=%async_computation.6 | async-start | bytes 131072 | tf_op jit(solution)/shard_map/psum | solution.py:67
  373.0 13.7 %copy-start = (f32[16,1024]{1,0:T(8,128)}, f32[16,1024]{1,0:T(8,128)S(1)}, u32[]{:S(2)}) copy-start(f32[16,1024]{1,0:T(8,128)S(1)} %convolution_subtract_fusion.2) | copy-start | bytes 196612
  381.7 141.7 %all-reduce.17.cloned.1.call-start = ((), (), s32[]{:S(2)}) async-start(), calls=%async_computation.7 | async-start | bytes 131072 | tf_op jit(solution)/shard_map/psum | solution.py:11
  386.6 53.4 %slice-start.1 = ((f32[16,1024]{1,0:T(8,128)}), f32[16,896]{1,0:T(8,128)S(1)}, s32[]{:S(2)}) async-start(f32[16,1024]{1,0:T(8,128)} %copy-done), calls=%async_computation.11 | async-start | bytes 114688 | tf_op jit(solution)/shard_map/slice | solution.py:122
  440.0 115.5 %reduce-scatter.9.cloned.1.call-start = ((), (), s32[]{:S(2)}) async-start(), calls=%async_computation.9 | async-start | bytes 294912 | tf_op jit(solution)/shard_map/reduce_scatter | solution.py:100
  440.7 82.7 %copy-start.8 = (f32[128,128]{1,0:T(8,128)S(1)}, f32[128,128]{1,0:T(8,128)}, u32[]{:S(2)}) copy-start(f32[128,128]{1,0:T(8,128)} %param.20) | copy-start | bytes 196612
  440.7 114.8 %copy-start.9 = (f32[16,1024]{1,0:T(8,128)S(1)}, f32[16,1024]{1,0:T(8,128)}, u32[]{:S(2)}) copy-start(f32[16,1024]{1,0:T(8,128)} %param.18) | copy-start | bytes 196612
  525.1 32.1 %copy-start.5 = (f32[128,128]{1,0:T(8,128)}, f32[128,128]{1,0:T(8,128)S(1)}, u32[]{:S(2)}) copy-start(f32[128,128]{1,0:T(8,128)S(1)} %get-tuple-element.18) | copy-start | bytes 196612
Sparse Core Ops, SparseCore 0:
  11.8 89.6 all-reduce.6
  105.8 57.6 all-reduce.8
  167.7 79.9 all-reduce.10
  250.5 29.6 reduce-scatter.6
  284.3 85.8 all-reduce.12
  381.8 57.4 all-reduce.14
  443.4 79.9 all-reduce.16
  525.8 29.6 reduce-scatter.8
where the time goes:
time: 565 us; the launch traced here: 564 us
  waiting for transfers between devices  449 us (79%)
  matrix products  36.6 us (6%)
  other arithmetic  32.3 us (6%)
  blocking collectives  26.5 us (5%)
  between operations  14.4 us (3%)
    psum x4, waiting for transfers between devices, from_root(): return lax.psum(kept, axis)  290 us
    psum x2, waiting for transfers between devices, summed_block(): rows_sum = lax.psum(partial_value, 'row')  98.4 us
    reduce_scatter x1, waiting for transfers between devices, per_device(): lax.psum_scatter(jnp.dot(solved_two.T, trail, preferred_element_type=jnp....  30.7 us
    reduce_scatter x1, waiting for transfers between devices, per_device(): lax.psum_scatter((jnp.dot(head_rows.T, row_two, preferred_element_type=jn...  30.3 us
    another operation x2, other arithmetic, inverse_lower(): return lax.linalg.triangular_solve(block, ident, left_side=True, lower=True)  19.6 us
    all_gather x1, blocking collectives, per_device(): lax.all_gather(row_two, 'row', axis=0, tiled=True)  13.5 us
    all_gather x1, blocking collectives, per_device(): lax.all_gather(row_one, 'row', axis=0, tiled=True)  13 us
  transfers between devices with their start and end apart: 8, of which 8 were waited for; matrix products, arithmetic and copies ran while one was open for 9% of the time, Pallas kernels for 0%

commit v1 on v0

--- a/solution.py
+++ b/solution.py
@@ -8,7 +8,7 @@
 
 def from_root(value, axis, source):
     kept = jnp.where(lax.axis_index(axis) == source, value, 0).astype(value.dtype)
-    return lax.psum(kept, axis)
+    return jnp.sum(lax.all_gather(kept, axis), axis=0)
 
 
 def halved_lower(matrix):

time: 565 us -> 538 us (0.952)
  waiting for transfers between devices: 449 us -> 415 us
  other arithmetic: 32.3 us -> 48.3 us
  matrix products: 36.6 us -> 25 us
    psum x4 -> x0, waiting for transfers between devices: 290 us -> none  [from_root(): return lax.psum(kept, axis)]
    all_gather x0 -> x4, waiting for transfers between devices: none -> 239 us  [from_root(): return jnp.sum(lax.all_gather(kept, axis), axis=0)]
    psum x2, waiting for transfers between devices: 98.4 us -> 116 us  [summed_block(): rows_sum = lax.psum(partial_value, 'row')]
    unnamed x0 -> x2, other arithmetic: none -> 13.4 us
where the time goes in v1:
time: 538 us
  waiting for transfers between devices  415 us (77%)
  other arithmetic  48.3 us (9%)
  blocking collectives  25.9 us (5%)
  matrix products  25 us (5%)
  between operations  14.4 us (3%)
  local copies, waits for them, and re-layouts  8.28 us (2%)
    all_gather x4, waiting for transfers between devices, from_root(): return jnp.sum(lax.all_gather(kept, axis), axis=0)  239 us
    psum x2, waiting for transfers between devices, summed_block(): rows_sum = lax.psum(partial_value, 'row')  116 us
    reduce_scatter x1, waiting for transfers between devices, per_device(): lax.psum_scatter(jnp.dot(solved_two.T, trail, preferred_element_type=jnp....  30.4 us
    reduce_scatter x1, waiting for transfers between devices, per_device(): lax.psum_scatter((jnp.dot(head_rows.T, row_two, preferred_element_type=jn...  30 us
    another operation x2, other arithmetic, inverse_lower(): return lax.linalg.triangular_solve(block, ident, left_side=True, lower=True)  19.6 us
    unnamed x2, other arithmetic  13.4 us
    all_gather x1, blocking collectives, per_device(): lax.all_gather(row_one, 'row', axis=0, tiled=True)  13 us
    all_gather x1, blocking collectives, per_device(): lax.all_gather(row_two, 'row', axis=0, tiled=True)  12.8 us
  transfers between devices with their start and end apart: 8, of which 8 were waited for; matrix products, arithmetic and copies ran while one was open for 9% of the time, Pallas kernels for 0%

profile of v1, /device:TPU:0, one launch (start us, length us, event | category | flops | bytes accessed | tf_op | source)
XLA Modules:
  0.0 537.7 jit_solution(13866430416754330291)
XLA Ops:
  7.2 0.0 all-gather.10.cloned.1.call-start
  7.2 2.3 slice_select_fusion.1
  9.5 0.0 all-gather.10.cloned.1.call-update
  9.5 0.0 all-reduce.3.cloned.1.call-start
  9.6 0.9 select_bitcast_fusion.1
  10.4 9.8 %custom-call.4 = f32[1,128,128]{1,2,0:T(8,128)S(1)} custom-call(f32[1,128,128]{2,1,0:T(8,128)S(1)} %select_bitcast_fusion.1), custom_call_target="InvertDiagBlocksLowerTriangular" | custom-call | tf_op jit(solution)/shard_map/triangular_solve/custom-call.1 | solution.py:24
  20.2 0.3 fusion.13
  20.5 104.2 %all-gather.10.cloned.1.call-done = f32[32768,128]{1,0:T(8,128)} async-done(((f32[2048,128]{1,0:T(8,128)}), f32[32768,128]{1,0:T(8,128)}) %all-gather.10.cloned.1.call-update) | async-done | bytes 16777232 | tf_op jit(solution)/shard_map/all_gather | solution.py:11
  124.7 6.6 %reduce_sum.36 = f32[2048,128]{1,0:T(8,128)S(1)} reduce(f32[16,2048,128]{2,1,0:T(8,128)} %bitcast.54, f32[]{:T(128)} %constant.29.clone.1), dimensions={0}, to_apply=%region_0.1 | reduce | flops 3932160 | bytes 17825796
  131.4 1.0 convolution_convert_fusion.1
  132.4 2.0 fusion.6
  134.4 0.0 all-gather.12.cloned.1.call-start
  134.5 58.3 %all-reduce.3.cloned.1.call-done = f32[128,128]{1,0:T(8,128)} async-done(((f32[128,128]{1,0:T(8,128)}), f32[128,128]{1,0:T(8,128)}) %all-reduce.3.cloned.1.call-update) | async-done | bytes 65552 | tf_op jit(solution)/shard_map/psum | solution.py:67
  192.7 0.6 broadcast_select_fusion.1
  193.4 0.0 reduce-scatter.7.cloned.1.call-start
  193.5 12.8 %all_gather.30 = bf16[128,1024]{1,0:T(8,128)(2,1)S(1)} all-gather(bf16[16,1024]{1,0:T(8,128)(2,1)S(1)} %copy-done.5), channel_id=1, replica_groups=mesh['row'=8,'col'=16] {'row'}, dimensions={0}, use_global_device_ids=true | all-gather | bytes 294912 | tf_op jit(solution)/shard_map/all_gather | solution.py:56
  206.3 3.6 convolution_convert_fusion.2
  210.0 4.7 convolution_subtract_fusion.1
  214.6 3.2 copy-done
  217.9 0.1 slice_bitcast_fusion
  218.0 0.0 reduce-scatter.7.cloned.1.call-update
  218.1 0.0 all-gather.8.cloned.1.call-start
  218.1 19.5 %all-gather.12.cloned.1.call-done = f32[2048,128]{1,0:T(8,128)} async-done(((f32[128,128]{1,0:T(8,128)}), f32[2048,128]{1,0:T(8,128)}) %all-gather.12.cloned.1.call-update) | async-done | bytes 1048592 | tf_op jit(solution)/shard_map/all_gather | solution.py:11
  237.6 1.3 reduce_sum.37
  238.9 0.3 fusion.2
  239.2 0.3 fusion.42
  239.5 0.2 fusion.25
  239.7 0.1 copy.57
  239.8 30.4 %reduce-scatter.7.cloned.1.call-done = bf16[16,1024]{1,0:T(8,128)(2,1)} async-done(((bf16[128,1024]{1,0:T(8,128)(2,1)}), bf16[16,1024]{1,0:T(8,128)(2,1)}) %reduce-scatter.7.cloned.1.call-update) | async-done | bytes 32784 | tf_op jit(solution)/shard_map/reduce_scatter | solution.py:78
  270.2 1.0 convolution_subtract_fusion.4
  271.2 1.0 maximum_select_fusion
  272.3 0.0 all-reduce.5.cloned.1.call-start
  272.4 9.8 %custom-call.5 = f32[1,128,128]{1,2,0:T(8,128)S(1)} custom-call(f32[1,128,128]{2,1,0:T(8,128)S(1)} %select_bitcast_fusion), custom_call_target="InvertDiagBlocksLowerTriangular" | custom-call | tf_op jit(solution)/shard_map/triangular_solve/custom-call.1 | solution.py:24
  282.2 13.0 %all_gather.34 = bf16[128,1024]{1,0:T(8,128)(2,1)S(1)} all-gather(bf16[16,1024]{1,0:T(8,128)(2,1)S(1)} %copy-done.12), channel_id=1, replica_groups=mesh['row'=8,'col'=16] {'row'}, dimensions={0}, use_global_device_ids=true | all-gather | bytes 294912 | tf_op jit(solution)/shard_map/all_gather | solution.py:55
  295.2 0.3 fusion.11
  295.5 88.4 %all-gather.8.cloned.1.call-done = f32[16,2064,128]{2,1,0:T(8,128)} async-done(((f32[1,2064,128]{2,1,0:T(8,128)}), f32[16,2064,128]{2,1,0:T(8,128)}) %all-gather.8.cloned.1.call-update) | async-done | bytes 16908304 | tf_op jit(solution)/shard_map/all_gather | solution.py:11
  383.9 6.7 %reduce_sum.38 = f32[2064,128]{1,0:T(8,128)S(1)} reduce(f32[16,2064,128]{2,1,0:T(8,128)} %all-gather.8.cloned.1.call-done, f32[]{:T(128)} %constant.29.clone.1), dimensions={0}, to_apply=%region_4.6 | reduce | flops 3962880 | bytes 17965060
  390.6 1.0 convolution_convert_fusion
  391.6 0.2 fusion.32
  391.8 2.0 convolution_add_fusion.1
  393.8 0.0 all-gather.14.cloned.1.call-start
  393.9 0.2 convolution_subtract_fusion.2
  394.0 58.1 %all-reduce.5.cloned.1.call-done = f32[128,128]{1,0:T(8,128)} async-done(((f32[128,128]{1,0:T(8,128)}), f32[128,128]{1,0:T(8,128)}) %all-reduce.5.cloned.1.call-update) | async-done | bytes 65552 | tf_op jit(solution)/shard_map/psum | solution.py:67
  452.2 0.6 broadcast_select_fusion
  452.8 0.0 reduce-scatter.9.cloned.1.call-start
  452.9 4.6 convolution_subtract_fusion
  457.5 2.0 copy-done.2
  459.5 2.3 slice.99
  461.8 0.6 pad_maximum_fusion.2
  462.5 0.2 fusion.36
  462.7 0.3 copy-done.1
  463.0 1.5 fusion
  464.5 1.2 fusion.4
  465.8 0.0 reduce-scatter.9.cloned.1.call-update
  465.8 4.7 pad_maximum_fusion
  470.5 26.5 %all-gather.14.cloned.1.call-done = f32[2048,128]{1,0:T(8,128)} async-done(((f32[128,128]{1,0:T(8,128)}), f32[2048,128]{1,0:T(8,128)}) %all-gather.14.cloned.1.call-update) | async-done | bytes 1048592 | tf_op jit(solution)/shard_map/all_gather | solution.py:11
  497.0 1.3 reduce_sum.39
  498.3 0.3 fusion.1
  498.6 0.3 fusion.43
  498.9 0.2 fusion.24
  499.1 0.1 copy.63
  499.2 30.0 %reduce-scatter.9.cloned.1.call-done = bf16[16,1024]{1,0:T(8,128)(2,1)} async-done(((bf16[128,1024]{1,0:T(8,128)(2,1)}), bf16[16,1024]{1,0:T(8,128)(2,1)}) %reduce-scatter.9.cloned.1.call-update) | async-done | bytes 32784 | tf_op jit(solution)/shard_map/reduce_scatter | solution.py:100
  529.2 1.0 convolution_subtract_fusion.3
  530.2 0.6 pad_maximum_fusion.1
  (35 shorter events, 0.2 us)
Async XLA Ops:
  7.2 117.6 %all-gather.10.cloned.1.call-start = ((), (), s32[]{:S(2)}) async-start(), calls=%async_computation.5 | async-start | bytes 17825792 | tf_op jit(solution)/shard_map/all_gather | solution.py:11
  9.5 183.2 %all-reduce.3.cloned.1.call-start = ((), (), s32[]{:S(2)}) async-start(), calls=%async_computation.2 | async-start | bytes 131072 | tf_op jit(solution)/shard_map/psum | solution.py:67
  124.7 68.7 %copy-start.5 = (bf16[16,1024]{1,0:T(8,128)(2,1)S(1)}, bf16[16,1024]{1,0:T(8,128)(2,1)}, u32[]{:S(2)}) copy-start(bf16[16,1024]{1,0:T(8,128)(2,1)} %param.14) | copy-start | bytes 98308
  134.4 103.2 %all-gather.12.cloned.1.call-start = ((), (), s32[]{:S(2)}) async-start(), calls=%async_computation.6 | async-start | bytes 1114112 | tf_op jit(solution)/shard_map/all_gather | solution.py:11
  193.4 76.8 %reduce-scatter.7.cloned.1.call-start = ((), (), s32[]{:S(2)}) async-start(), calls=%async_computation.8 | async-start | bytes 294912 | tf_op jit(solution)/shard_map/reduce_scatter | solution.py:78
  210.0 28.9 %copy-start.3 = (f32[128,128]{1,0:T(8,128)S(1)}, f32[128,128]{1,0:T(8,128)}, u32[]{:S(2)}) copy-start(f32[128,128]{1,0:T(8,128)} %param.16) | copy-start | bytes 196612
  210.0 28.9 %copy-start.8 = (f32[128,128]{1,0:T(8,128)S(1)}, f32[128,128]{1,0:T(8,128)}, u32[]{:S(2)}) copy-start(f32[128,128]{1,0:T(8,128)} %param.21) | copy-start | bytes 196612
  214.6 3.3 copy-start
  217.9 52.4 %copy-start.9 = (f32[16,1024]{1,0:T(8,128)S(1)}, f32[16,1024]{1,0:T(8,128)}, u32[]{:S(2)}) copy-start(f32[16,1024]{1,0:T(8,128)} %param.19) | copy-start | bytes 196612
  217.9 54.5 %copy-start.4 = (f32[128,128]{1,0:T(8,128)S(1)}, f32[128,128]{1,0:T(8,128)}, u32[]{:S(2)}) copy-start(f32[128,128]{1,0:T(8,128)} %param.15) | copy-start | bytes 196612
  217.9 64.3 %copy-start.12 = (bf16[16,1024]{1,0:T(8,128)(2,1)S(1)}, bf16[16,1024]{1,0:T(8,128)(2,1)}, u32[]{:S(2)}) copy-start(bf16[16,1024]{1,0:T(8,128)(2,1)} %param.13) | copy-start | bytes 98308
  218.1 165.8 %all-gather.8.cloned.1.call-start = ((), (), s32[]{:S(2)}) async-start(), calls=%async_computation.3 | async-start | bytes 17965056 | tf_op jit(solution)/shard_map/all_gather | solution.py:11
  239.7 150.9 %copy-start.6 = (f32[128,128]{1,0:T(8,128)}, f32[128,128]{1,0:T(8,128)S(1)}, u32[]{:S(2)}) copy-start(f32[128,128]{1,0:T(8,128)S(1)} %get-tuple-element.16) | copy-start | bytes 196612
  272.3 179.9 %all-reduce.5.cloned.1.call-start = ((), (), s32[]{:S(2)}) async-start(), calls=%async_computation.4 | async-start | bytes 131072 | tf_op jit(solution)/shard_map/psum | solution.py:67
  393.8 103.2 %all-gather.14.cloned.1.call-start = ((), (), s32[]{:S(2)}) async-start(), calls=%async_computation.7 | async-start | bytes 1114112 | tf_op jit(solution)/shard_map/all_gather | solution.py:11
  452.8 76.4 %reduce-scatter.9.cloned.1.call-start = ((), (), s32[]{:S(2)}) async-start(), calls=%async_computation.9 | async-start | bytes 294912 | tf_op jit(solution)/shard_map/reduce_scatter | solution.py:100
  457.5 2.0 copy-start.2
  459.5 3.5 copy-start.1
  465.8 32.5 %copy-start.10 = (f32[128,128]{1,0:T(8,128)S(1)}, f32[128,128]{1,0:T(8,128)}, u32[]{:S(2)}) copy-start(f32[128,128]{1,0:T(8,128)} %param.20) | copy-start | bytes 196612
  465.8 63.4 %copy-start.11 = (f32[16,1024]{1,0:T(8,128)S(1)}, f32[16,1024]{1,0:T(8,128)}, u32[]{:S(2)}) copy-start(f32[16,1024]{1,0:T(8,128)} %param.18) | copy-start | bytes 196612
  499.1 31.7 %copy-start.7 = (f32[128,128]{1,0:T(8,128)}, f32[128,128]{1,0:T(8,128)S(1)}, u32[]{:S(2)}) copy-start(f32[128,128]{1,0:T(8,128)S(1)} %get-tuple-element.18) | copy-start | bytes 196612
Sparse Core Ops, SparseCore 0:
  10.7 113.9 all-gather.9
  134.5 58.1 all-reduce.2
  195.7 41.8 all-gather.11
  240.5 29.6 reduce-scatter.6
  272.8 111.0 all-gather.7
  394.0 58.1 all-reduce.4
  455.1 41.8 all-gather.13
  499.5 29.6 reduce-scatter.8
